TPU v7x, 128 devices: a whole 4x4x4 slice. The times are simulated.
128 devices in a mesh: cell: 2 (over core), panel: 2 (over x_lo), sc: 32 (over z, y, x_hi).
Axes of the slice: x: 4 (x_hi: 2, x_lo: 2; x = x_hi * 2 + x_lo), y: 4, z: 4, core: 2. Of those that a mesh axis runs over, the one named last changes fastest.
Arguments:
- channel: bfloat16 [4, 1024, 2, 1024, 128], P('cell', 'sc', None, 'panel'), may hold values from -0.1875 to 0.1875
- received: bfloat16 [4, 1024, 2, 14, 1024], P('cell', 'sc', None, None, 'panel'), may hold values from -6 to 6
- noise_power: float32 [4], P('cell'), may hold values from 0.05 to 0.5
- user_count: int32 [4, 64], P('cell', 'sc'), may hold values from 32 to 128
- serving_cell: int32 [4, 128, 1], P('cell'), may hold values from 0 to 3; in each aligned block of 256 rows (0 to 255, 256 to 511, ..., all dimensions but the last counted through in order) at most 128 rows name the same one
Outputs:
- routed_symbols: bfloat16 [4, 256, 2, 14, 1024], P('cell', 'sc')
Inputs may be any that keep to these rules, and one draw needn't show every extreme that they name: `serving_cell`: at most 128 user slots of one block of 2 consecutive cells name the same serving cell, and in every draw some serving cell is named exactly 128 times by one block.
All inputs are finite; a program needn't handle non-finite values.
Results may differ from a plain program's by a relative error of at most 0.0057.
Values may be sent and summed in bfloat16 or wider, within the bound.
A program may use at most 128 MiB of HBM per device.

v0:
```python
import jax
import jax.numpy as jnp
from jax import lax
from jax.sharding import PartitionSpec as P

GRP = 16
ITERS = 2


def with_halo(block, sides, width):
    for axis, dim in sides:
        count = lax.axis_size(axis)
        forward = [(i, i + 1) for i in range(count - 1)]
        backward = [(target, source) for source, target in forward]
        low = lax.ppermute(
            lax.slice_in_dim(block, block.shape[dim] - width, None, axis=dim), axis, forward
        )
        high = lax.ppermute(lax.slice_in_dim(block, 0, width, axis=dim), axis, backward)
        block = jnp.concatenate([low, block, high], axis=dim)
    return block


def adjoint_apply(matrix, vector):
    products = jnp.einsum("cfaku,cfbsk->cfabsu", matrix, vector, preferred_element_type=jnp.float32)
    return jnp.stack(
        (products[:, :, 0, 0] + products[:, :, 1, 1], products[:, :, 0, 1] - products[:, :, 1, 0]),
        axis=2,
    )


def apply_channel(matrix, vector):
    products = jnp.einsum("cfaku,cfbsu->cfabsk", matrix, vector, preferred_element_type=jnp.float32)
    return jnp.stack(
        (products[:, :, 0, 0] - products[:, :, 1, 1], products[:, :, 0, 1] + products[:, :, 1, 0]),
        axis=2,
    )


def user_sum(left, right):
    return jnp.sum(left * right, axis=(2, 4))


def widen(values):
    return values[:, :, None, :, None]


def body(channel, received, noise_power, user_count, serving_cell):
    cells, band, _, antennas, users = channel.shape
    padded = with_halo(channel, (("sc", 1),), 1)
    total = band * lax.axis_size("sc")
    index = lax.axis_index("sc") * band + lax.iota(jnp.int32, band)
    weight = jnp.where((index == 0) | (index == total - 1), 0.75, 1.0).astype(jnp.float32)
    lower = padded[:, :-2].astype(jnp.float32)
    middle = padded[:, 1:-1].astype(jnp.float32)
    upper = padded[:, 2:].astype(jnp.float32)
    smooth = (0.25 * lower + 0.5 * middle + 0.25 * upper) / weight[None, :, None, None, None]
    counts = jnp.repeat(user_count, GRP, axis=1)
    active = (lax.iota(jnp.int32, users)[None, None, :] < counts[:, :, None]).astype(jnp.float32)
    smoothed = (smooth * active[:, :, None, None, :]).astype(jnp.bfloat16)
    partial_sums = adjoint_apply(smoothed, received)
    noise = noise_power[:, None, None, None, None]
    matched = lax.psum(partial_sums, "panel")
    estimate = jnp.zeros_like(matched)
    residual = matched
    direction = matched
    norm_now = user_sum(residual, residual)
    for iteration in range(ITERS):
        column_image = apply_channel(smoothed, direction.astype(jnp.bfloat16)).astype(jnp.bfloat16)
        image = lax.psum(adjoint_apply(smoothed, column_image), "panel") + noise * direction
        alpha = norm_now / user_sum(direction, image)
        estimate = estimate + widen(alpha) * direction
        residual = residual - widen(alpha) * image
        norm_next = user_sum(residual, residual)
        direction = residual + widen(norm_next / norm_now) * direction
        norm_now = norm_next
    detected = estimate.astype(jnp.bfloat16)
    n_cell = lax.axis_size("cell")
    capacity = 2 * users // n_cell
    slot_count = n_cell * capacity
    keys = serving_cell[:, :, 0].reshape(-1)
    position = lax.iota(jnp.int32, cells * users)
    earlier = (keys[:, None] == keys[None, :]) & (position[None, :] < position[:, None])
    rank = jnp.sum(earlier.astype(jnp.int32), axis=1)
    target = keys % cells * slot_count + keys // cells * capacity + rank
    onehot = (target[:, None] == lax.iota(jnp.int32, cells * slot_count)[None, :]).astype(
        jnp.bfloat16
    )
    onehot = onehot.reshape(cells, users, cells * slot_count)
    outgoing = jnp.einsum("cfasu,cut->tasf", detected, onehot, preferred_element_type=jnp.float32)
    outgoing = outgoing.astype(jnp.bfloat16).reshape(cells, slot_count, 2, detected.shape[3], band)
    return lax.all_to_all(
        lax.all_to_all(outgoing, "cell", split_axis=1, concat_axis=1, tiled=True),
        "sc",
        split_axis=1,
        concat_axis=4,
        tiled=True,
    )


def solution(mesh):
    return jax.shard_map(
        body,
        mesh=mesh,
        in_specs=(
            P("cell", "sc", None, "panel", None),
            P("cell", "sc", None, None, "panel"),
            P("cell"),
            P("cell", "sc"),
            P("cell", None, None),
        ),
        out_specs=P("cell", "sc", None, None, None),
        check_vma=False,
    )
```

profile of v0, /device:TPU:0, one launch (start us, length us, event | category | flops | bytes accessed | tf_op | source)
XLA Modules:
  0.0 358.8 jit_solution(6481282010595207241)
XLA Ops:
  8.7 5.1 %collective-permute-start = (bf16[2,1,2,512,128]{4,3,2,1,0:T(8,128)(2,1)}, bf16[2,1,2,512,128]{4,3,2,1,0:T(8,128)(2,1)S(1)}, u32[]{:S(2)}, u32[]{:S(2)}) collective-permute-start(bf16[2,1,2,512,128]{4,3,2,1,0:T(8,128)(2,1)} %get-tuple-element.7), channel_id=1, source_target_pairs={{0,1},{1,2},{2,3},{3,4},{4,5},{5,6},{6,7},{7,8},{8,9},{9,10},{10,1... | collective-permute-start | bytes 1572872 | tf_op jit(solution)/shard_map/ppermute | solution.py:15
  16.0 9.2 %collective-permute-done = bf16[2,1,2,512,128]{4,3,2,1,0:T(8,128)(2,1)S(1)} collective-permute-done((bf16[2,1,2,512,128]{4,3,2,1,0:T(8,128)(2,1)}, bf16[2,1,2,512,128]{4,3,2,1,0:T(8,128)(2,1)S(1)}, u32[]{:S(2)}, u32[]{:S(2)}) %collective-permute-start) | collective-permute-done | bytes 524320 | tf_op jit(solution)/shard_map/ppermute | solution.py:15
  25.3 13.1 %collective-permute-done.1 = bf16[2,1,2,512,128]{4,3,2,1,0:T(8,128)(2,1)S(1)} collective-permute-done((bf16[2,1,2,512,128]{4,3,2,1,0:T(8,128)(2,1)S(1)}, bf16[2,1,2,512,128]{4,3,2,1,0:T(8,128)(2,1)S(1)}, u32[]{:S(2)}, u32[]{:S(2)}) %collective-permute-start.1) | collective-permute-done | bytes 524320 | tf_op jit(solution)/shard_map/ppermute | solution.py:18
  38.4 26.0 %multiply_convert_fusion = bf16[2,32,2,512,128]{4,3,2,1,0:T(8,128)(2,1)} fusion(bf16[2,32,2,512,128]{4,3,2,1,0:T(8,128)(2,1)} %param.5, bf16[2,1,2,512,128]{4,3,2,1,0:T(8,128)(2,1)S(1)} %collective-permute-done.1, bf16[2,1,2,512,128]{4,3,2,1,0:T(8,128)(2,1)S(1)} %collective-permute-done, f32[2,32,128]{2,1,0:T(8,128)S(1)} %fusion.44, f32[32]{0:T(128)S(1)} %or_select_fusion), kind=kLoop, calls=%fused_computation | loop fusion | flops 109051904 | bytes 34635904 | tf_op jit(solution)/shard_map/convert_element_type | solution.py:59
  64.4 7.0 %fusion = f32[2,32,2,128,2,14]{3,5,4,2,1,0:T(8,128)S(1)} fusion(bf16[2,32,2,512,128]{4,3,2,1,0:T(8,128)(2,1)} %multiply_convert_fusion, bf16[2,32,2,14,512,1]{4,2,3,1,0,5:T(2,128)(2,1)S(1)} %bitcast.138), kind=kOutput, calls=%fused_computation.3 | convolution fusion | flops 469762048 | bytes 20447232 | tf_op jit(solution)/shard_map/cfaku,cfbsk->cfabsu/dot_general | solution.py:24
  73.9 45.8 %all-reduce.4.cloned.1.call-done = f32[2,32,2,14,128]{4,1,3,2,0:T(8,128)} async-done(((f32[2,32,2,14,128]{4,1,3,2,0:T(8,128)}), f32[2,32,2,14,128]{4,1,3,2,0:T(8,128)}) %all-reduce.4.cloned.1.call-update) | async-done | bytes 917520 | tf_op jit(solution)/shard_map/psum | solution.py:62
  120.9 14.8 %fusion.10 = f32[2,32,2,2,14,512]{5,4,2,3,1,0:T(8,128)} fusion(bf16[2,32,2,512,128]{4,3,2,1,0:T(8,128)(2,1)} %multiply_convert_fusion, bf16[2,32,2,14,128,1]{4,1,3,2,0,5:T(8,128)(2,1)S(1)} %convert_bitcast_fusion.1), kind=kOutput, calls=%fused_computation.14 | convolution fusion | flops 469762048 | bytes 24576000 | tf_op jit(solution)/shard_map/cfaku,cfbsu->cfabsk/dot_general | solution.py:32
  135.8 2.6 fusion.26
  141.0 8.2 %fusion.6 = f32[2,32,2,14,2,128]{5,3,4,2,1,0:T(8,128)S(1)} fusion(bf16[2,32,2,512,128]{4,3,2,1,0:T(8,128)(2,1)} %multiply_convert_fusion, bf16[2,32,1,14,512]{4,3,1,0,2:T(8,128)(2,1)S(1)} %fusion.27, bf16[2,32,1,14,512]{4,3,1,0,2:T(8,128)(2,1)S(1)} %fusion.26), kind=kOutput, calls=%fused_computation.9 | convolution fusion | flops 470679552 | bytes 20447232 | tf_op jit(solution)/shard_map/cfaku,cfbsk->cfabsu/dot_general | solution.py:24
  151.8 44.6 %all-reduce.6.cloned.1.call-done = f32[2,32,2,14,128]{4,1,3,2,0:T(8,128)} async-done(((f32[2,32,2,14,128]{4,1,3,2,0:T(8,128)}), f32[2,32,2,14,128]{4,1,3,2,0:T(8,128)}) %all-reduce.6.cloned.1.call-update) | async-done | bytes 917520 | tf_op jit(solution)/shard_map/psum | solution.py:69
  200.2 14.8 %fusion.13 = f32[2,32,2,2,14,512]{5,4,2,3,1,0:T(8,128)} fusion(bf16[2,32,2,512,128]{4,3,2,1,0:T(8,128)(2,1)} %multiply_convert_fusion, bf16[2,32,2,14,128,1]{4,1,3,2,0,5:T(8,128)(2,1)S(1)} %convert_bitcast_fusion), kind=kOutput, calls=%fused_computation.15 | convolution fusion | flops 469762048 | bytes 24576000 | tf_op jit(solution)/shard_map/cfaku,cfbsu->cfabsk/dot_general | solution.py:32
  220.3 8.2 %fusion.2 = f32[2,32,2,14,2,128]{5,3,4,2,1,0:T(8,128)S(1)} fusion(bf16[2,32,2,512,128]{4,3,2,1,0:T(8,128)(2,1)} %multiply_convert_fusion, bf16[2,32,1,14,512]{4,3,1,0,2:T(8,128)(2,1)S(1)} %fusion.29, bf16[2,32,1,14,512]{4,3,1,0,2:T(8,128)(2,1)S(1)} %fusion.28), kind=kOutput, calls=%fused_computation.5 | convolution fusion | flops 470679552 | bytes 20447232 | tf_op jit(solution)/shard_map/cfaku,cfbsk->cfabsu/dot_general | solution.py:24
  231.0 44.7 %all-reduce.8.cloned.1.call-done = f32[2,32,2,14,128]{4,1,3,2,0:T(8,128)} async-done(((f32[2,32,2,14,128]{4,1,3,2,0:T(8,128)}), f32[2,32,2,14,128]{4,1,3,2,0:T(8,128)}) %all-reduce.8.cloned.1.call-update) | async-done | bytes 917520 | tf_op jit(solution)/shard_map/psum | solution.py:69
  278.4 7.0 %copy.123 = bf16[2,256,2,14,32]{4,2,3,0,1:T(2,128)(2,1)} copy(bf16[2,256,2,14,32]{1,0,4,3,2:T(2,128)(2,1)S(1)} %reshape.282) | data formatting | bytes 1835008 | tf_op jit(solution)/shard_map/reshape | solution.py:90
  285.4 5.1 %reshape.292 = bf16[2,2,114688]{2,1,0:T(2,128)(2,1)S(1)} reshape(bf16[256,2,14,2,32]{4,3,2,1,0:T(2,128)(2,1)} %bitcast.141) | data formatting | bytes 1835008
  290.5 4.5 %all_to_all.23 = bf16[2,2,114688]{2,1,0:T(2,128)(2,1)S(1)} all-to-all(bf16[2,2,114688]{2,1,0:T(2,128)(2,1)S(1)} %reshape.292), channel_id=1, replica_groups=mesh['cell'=2,'panel'=2,'sc'=32] {'cell'}, dimensions={0} | all-to-all | bytes 1835008 | tf_op jit(solution)/shard_map/all_to_all | solution.py:92
  294.9 3.0 reshape.293
  297.9 6.3 %bitcast_bitcast_fusion = bf16[256,2,14,2,32]{4,3,2,1,0:T(2,128)(2,1)} fusion(bf16[256,2,14,2,32]{4,3,2,1,0:T(2,128)(2,1)} %reshape.293), kind=kLoop, calls=%fused_computation.89 | loop fusion | bytes 1835008
  304.3 5.0 %reshape.294 = bf16[32,2,7168]{2,1,0:T(2,128)(2,1)S(1)} reshape(bf16[256,2,14,2,32]{4,3,2,1,0:T(2,128)(2,1)} %bitcast_bitcast_fusion) | data formatting | bytes 1835008
  309.3 27.6 %all_to_all.24 = bf16[32,2,7168]{2,1,0:T(2,128)(2,1)S(1)} all-to-all(bf16[32,2,7168]{2,1,0:T(2,128)(2,1)S(1)} %reshape.294), channel_id=1, replica_groups=mesh['cell'=2,'panel'=2,'sc'=32] {'sc'}, dimensions={0} | all-to-all | bytes 1835008 | tf_op jit(solution)/shard_map/all_to_all | solution.py:91
  336.8 3.2 reshape.295
  340.1 2.9 copy.166
  343.0 2.8 copy.146
  345.8 6.5 %reshape.291 = bf16[2,8,2,14,1024]{4,2,3,1,0:T(2,128)(2,1)} reshape(bf16[2,8,2,14,32,32]{5,4,2,3,1,0:T(8,128)(2,1)} %copy.146) | data formatting | bytes 1835008 | tf_op jit(solution)/shard_map/all_to_all | solution.py:91
  (48 shorter events, 27.3 us)
Async XLA Ops:
  6.5 57.8 %copy-start = (bf16[2,32,2,14,512]{4,2,3,1,0:T(2,128)(2,1)S(1)}, bf16[2,32,2,14,512]{4,2,3,1,0:T(2,128)(2,1)}, u32[]{:S(2)}) copy-start(bf16[2,32,2,14,512]{4,2,3,1,0:T(2,128)(2,1)} %param.6) | copy-start | bytes 5505028
  6.5 113.2 %all-reduce.4.cloned.1.call-start = ((), (), s32[]{:S(2)}) async-start(), calls=%async_computation.2 | async-start | bytes 1835008 | tf_op jit(solution)/shard_map/psum | solution.py:62
  8.7 16.5 %collective-permute-start = (bf16[2,1,2,512,128]{4,3,2,1,0:T(8,128)(2,1)}, bf16[2,1,2,512,128]{4,3,2,1,0:T(8,128)(2,1)S(1)}, u32[]{:S(2)}, u32[]{:S(2)}) collective-permute-start(bf16[2,1,2,512,128]{4,3,2,1,0:T(8,128)(2,1)} %get-tuple-element.7), channel_id=1, source_target_pairs={{0,1},{1,2},{2,3},{3,4},{4,5},{5,6},{6,7},{7,8},{8,9},{9,10},{10,1... | collective-permute-start | bytes 1572872 | tf_op jit(solution)/shard_map/ppermute | solution.py:15
  13.8 24.6 %collective-permute-start.1 = (bf16[2,1,2,512,128]{4,3,2,1,0:T(8,128)(2,1)S(1)}, bf16[2,1,2,512,128]{4,3,2,1,0:T(8,128)(2,1)S(1)}, u32[]{:S(2)}, u32[]{:S(2)}) collective-permute-start(bf16[2,1,2,512,128]{4,3,2,1,0:T(8,128)(2,1)S(1)} %get-tuple-element.8), channel_id=1, source_target_pairs={{1,0},{2,1},{3,2},{4,3},{5,4},{6,5},{7,6},{8,7},{9,8},{10,9},{11,1... | collective-permute-start | bytes 1572872 | tf_op jit(solution)/shard_map/ppermute | solution.py:18
  73.7 122.8 %all-reduce.6.cloned.1.call-start = ((), (), s32[]{:S(2)}) async-start(), calls=%async_computation.3 | async-start | bytes 1835008 | tf_op jit(solution)/shard_map/psum | solution.py:69
  150.3 46.1 %copy-start.2 = (f32[2,32,2,14,128]{4,1,3,2,0:T(8,128)S(1)}, f32[2,32,2,14,128]{4,1,3,2,0:T(8,128)}, u32[]{:S(2)}) copy-start(f32[2,32,2,14,128]{4,1,3,2,0:T(8,128)} %all-reduce.4.cloned.1.call-done) | copy-start | bytes 2752516
  150.3 46.1 %copy-start.5 = (f32[2]{0:T(128)S(1)}, f32[2]{0:T(128)}, u32[]{:S(2)}) copy-start(f32[2]{0:T(128)} %param.7) | copy-start | bytes 28
  151.5 124.1 %all-reduce.8.cloned.1.call-start = ((), (), s32[]{:S(2)}) async-start(), calls=%async_computation.4 | async-start | bytes 1835008 | tf_op jit(solution)/shard_map/psum | solution.py:69
  196.4 3.3 copy-start.3
  229.5 1.2 copy-start.4
  343.0 9.3 %copy-start.1 = (bf16[2,32,2,14,512]{4,2,3,1,0:T(2,128)(2,1)S(1)}, bf16[2,32,2,14,512]{4,2,3,1,0:T(2,128)(2,1)}, u32[]{:S(2)}) copy-start(bf16[2,32,2,14,512]{4,2,3,1,0:T(2,128)(2,1)} %param.6) | copy-start | bytes 5505028
Sparse Core Ops, SparseCore 0:
  73.8 45.8 all-reduce.3
  151.6 44.7 all-reduce.5
  230.9 44.7 all-reduce.7
where the time goes:
time: 360 us; the launch traced here: 359 us
  waiting for transfers between devices  158 us (44%)
  matrix products  53.8 us (15%)
  local copies, waits for them, and re-layouts  48.4 us (13%)
  other arithmetic  46.9 us (13%)
  blocking collectives  32 us (9%)
  between operations  13.4 us (4%)
  starting transfers between devices  6.84 us (2%)
    psum x2, waiting for transfers between devices, body(): lax.psum(adjoint_apply(smoothed, column_image), 'panel') + noise * direction  89.4 us
    psum x1, waiting for transfers between devices, body(): matched = lax.psum(partial_sums, 'panel')  45.8 us
    dot_general x2, matrix products, apply_channel(): jnp.einsum('cfaku,cfbsu->cfabsk', matrix, vector, preferred_element_type=...  29.7 us
    all_to_all x1, blocking collectives, body(): lax.all_to_all(lax.all_to_all(outgoing, 'cell', split_axis=1, concat_axis...  27.6 us
    convert_element_type x1, other arithmetic, body(): smoothed = (smooth * active[:, :, None, None, :]).astype(jnp.bfloat16)  26 us
    dot_general x3, matrix products, adjoint_apply(): jnp.einsum('cfaku,cfbsk->cfabsu', matrix, vector, preferred_element_type=...  23.4 us
    unnamed x17, local copies, waits for them, and re-layouts  22.7 us
    ppermute x1, waiting for transfers between devices, with_halo(): lax.ppermute(lax.slice_in_dim(block, 0, width, axis=dim), axis, backward)  13.1 us
  transfers between devices with their start and end apart: 5, of which 5 were waited for; matrix products, arithmetic and copies ran while one was open for 0% of the time, Pallas kernels for 0%

commit v1 on v0

--- a/solution.py
+++ b/solution.py
@@ -66,7 +66,10 @@
     norm_now = user_sum(residual, residual)
     for iteration in range(ITERS):
         column_image = apply_channel(smoothed, direction.astype(jnp.bfloat16)).astype(jnp.bfloat16)
-        image = lax.psum(adjoint_apply(smoothed, column_image), "panel") + noise * direction
+        image = (
+            jnp.sum(lax.all_gather(adjoint_apply(smoothed, column_image), "panel"), axis=0)
+            + noise * direction
+        )
         alpha = norm_now / user_sum(direction, image)
         estimate = estimate + widen(alpha) * direction
         residual = residual - widen(alpha) * image

time: 360 us -> 347 us (0.964)
  waiting for transfers between devices: 158 us -> 141 us
    psum x2 -> x0, waiting for transfers between devices: 89.4 us -> none  [body(): lax.psum(adjoint_apply(smoothed, column_image), 'panel') + noise * direction]
    all_gather x0 -> x2, waiting for transfers between devices: none -> 73 us  [body(): lax.all_gather(adjoint_apply(smoothed, column_image), 'panel')]
    reduce_sum x0 -> x2, other arithmetic: none -> 4.74 us  [body(): jnp.sum(lax.all_gather(adjoint_apply(smoothed, column_image), 'panel'), a...]
    unnamed x17 -> x15, local copies, waits for them, and re-layouts: 22.7 us -> 22.6 us
where the time goes in v1:
time: 347 us; the launch traced here: 346 us
  waiting for transfers between devices  141 us (41%)
  matrix products  54.8 us (16%)
  other arithmetic  50 us (14%)
  local copies, waits for them, and re-layouts  48.4 us (14%)
  blocking collectives  31.9 us (9%)
  between operations  13.4 us (4%)
  starting transfers between devices  6.62 us (2%)
    all_gather x2, waiting for transfers between devices, body(): lax.all_gather(adjoint_apply(smoothed, column_image), 'panel')  73 us
    psum x1, waiting for transfers between devices, body(): matched = lax.psum(partial_sums, 'panel')  46 us
    dot_general x2, matrix products, apply_channel(): jnp.einsum('cfaku,cfbsu->cfabsk', matrix, vector, preferred_element_type=...  29.7 us
    all_to_all x1, blocking collectives, body(): lax.all_to_all(lax.all_to_all(outgoing, 'cell', split_axis=1, concat_axis...  27.4 us
    convert_element_type x1, other arithmetic, body(): smoothed = (smooth * active[:, :, None, None, :]).astype(jnp.bfloat16)  26 us
    dot_general x3, matrix products, adjoint_apply(): jnp.einsum('cfaku,cfbsk->cfabsu', matrix, vector, preferred_element_type=...  23.4 us
    unnamed x15, local copies, waits for them, and re-layouts  22.6 us
    ppermute x1, waiting for transfers between devices, with_halo(): lax.ppermute(lax.slice_in_dim(block, 0, width, axis=dim), axis, backward)  13.1 us
  transfers between devices with their start and end apart: 5, of which 5 were waited for; matrix products, arithmetic and copies ran while one was open for 0% of the time, Pallas kernels for 0%

profile of v1, /device:TPU:0, one launch (start us, length us, event | category | flops | bytes accessed | tf_op | source)
XLA Modules:
  0.0 346.5 jit_solution(10945824700965465879)
XLA Ops:
  8.7 5.1 %collective-permute-start = (bf16[2,1,2,512,128]{4,3,2,1,0:T(8,128)(2,1)}, bf16[2,1,2,512,128]{4,3,2,1,0:T(8,128)(2,1)S(1)}, u32[]{:S(2)}, u32[]{:S(2)}) collective-permute-start(bf16[2,1,2,512,128]{4,3,2,1,0:T(8,128)(2,1)} %get-tuple-element.7), channel_id=1, source_target_pairs={{0,1},{1,2},{2,3},{3,4},{4,5},{5,6},{6,7},{7,8},{8,9},{9,10},{10,1... | collective-permute-start | bytes 1572872 | tf_op jit(solution)/shard_map/ppermute | solution.py:15
  16.0 9.2 %collective-permute-done = bf16[2,1,2,512,128]{4,3,2,1,0:T(8,128)(2,1)S(1)} collective-permute-done((bf16[2,1,2,512,128]{4,3,2,1,0:T(8,128)(2,1)}, bf16[2,1,2,512,128]{4,3,2,1,0:T(8,128)(2,1)S(1)}, u32[]{:S(2)}, u32[]{:S(2)}) %collective-permute-start) | collective-permute-done | bytes 524320 | tf_op jit(solution)/shard_map/ppermute | solution.py:15
  25.3 13.1 %collective-permute-done.1 = bf16[2,1,2,512,128]{4,3,2,1,0:T(8,128)(2,1)S(1)} collective-permute-done((bf16[2,1,2,512,128]{4,3,2,1,0:T(8,128)(2,1)S(1)}, bf16[2,1,2,512,128]{4,3,2,1,0:T(8,128)(2,1)S(1)}, u32[]{:S(2)}, u32[]{:S(2)}) %collective-permute-start.1) | collective-permute-done | bytes 524320 | tf_op jit(solution)/shard_map/ppermute | solution.py:18
  38.4 26.0 %multiply_convert_fusion = bf16[2,32,2,512,128]{4,3,2,1,0:T(8,128)(2,1)} fusion(bf16[2,32,2,512,128]{4,3,2,1,0:T(8,128)(2,1)} %param.5, bf16[2,1,2,512,128]{4,3,2,1,0:T(8,128)(2,1)S(1)} %collective-permute-done.1, bf16[2,1,2,512,128]{4,3,2,1,0:T(8,128)(2,1)S(1)} %collective-permute-done, f32[2,32,128]{2,1,0:T(8,128)S(1)} %fusion.58, f32[32]{0:T(128)S(1)} %or_select_fusion), kind=kLoop, calls=%fused_computation | loop fusion | flops 109051904 | bytes 34635904 | tf_op jit(solution)/shard_map/convert_element_type | solution.py:59
  64.4 7.0 %fusion = f32[2,32,2,128,2,14]{3,5,4,2,1,0:T(8,128)S(1)} fusion(bf16[2,32,2,512,128]{4,3,2,1,0:T(8,128)(2,1)} %multiply_convert_fusion, bf16[2,32,2,14,512,1]{4,2,3,1,0,5:T(2,128)(2,1)S(1)} %bitcast.158), kind=kOutput, calls=%fused_computation.3 | convolution fusion | flops 469762048 | bytes 20447232 | tf_op jit(solution)/shard_map/cfaku,cfbsk->cfabsu/dot_general | solution.py:24
  73.7 46.0 %all-reduce.2.cloned.1.call-done = f32[2,32,2,14,128]{4,1,3,2,0:T(8,128)} async-done(((f32[2,32,2,14,128]{4,1,3,2,0:T(8,128)}), f32[2,32,2,14,128]{4,1,3,2,0:T(8,128)}) %all-reduce.2.cloned.1.call-update) | async-done | bytes 917520 | tf_op jit(solution)/shard_map/psum | solution.py:62
  120.9 14.8 %fusion.10 = f32[2,32,2,2,14,512]{5,4,2,3,1,0:T(8,128)} fusion(bf16[2,32,2,512,128]{4,3,2,1,0:T(8,128)(2,1)} %multiply_convert_fusion, bf16[2,32,2,14,128,1]{4,1,3,2,0,5:T(8,128)(2,1)S(1)} %convert_bitcast_fusion.1), kind=kOutput, calls=%fused_computation.14 | convolution fusion | flops 469762048 | bytes 24576000 | tf_op jit(solution)/shard_map/cfaku,cfbsu->cfabsk/dot_general | solution.py:32
  141.0 8.2 %fusion.25 = f32[2,32,2,2,14,128]{5,4,2,3,1,0:T(8,128)S(1)} fusion(bf16[2,32,2,512,128]{4,3,2,1,0:T(8,128)(2,1)} %multiply_convert_fusion, bf16[2,32,1,14,512]{4,3,1,0,2:T(8,128)(2,1)S(1)} %fusion.37, bf16[2,32,1,14,512]{4,3,1,0,2:T(8,128)(2,1)S(1)} %fusion.36), kind=kOutput, calls=%fused_computation.35 | convolution fusion | flops 470679552 | bytes 20447232 | tf_op jit(solution)/shard_map/cfaku,cfbsk->cfabsu/dot_general | solution.py:24
  150.7 36.5 %all-gather.5.cloned.1.call-done = f32[4,32,2,14,128]{4,3,1,0,2:T(8,128)} async-done(((f32[2,32,2,14,128]{4,3,1,0,2:T(8,128)}), f32[4,32,2,14,128]{4,3,1,0,2:T(8,128)}) %all-gather.5.cloned.1.call-update) | async-done | bytes 1835024 | tf_op jit(solution)/shard_map/all_gather | solution.py:70
  190.7 14.8 %fusion.13 = f32[2,32,2,2,14,512]{5,4,2,3,1,0:T(8,128)} fusion(bf16[2,32,2,512,128]{4,3,2,1,0:T(8,128)(2,1)} %multiply_convert_fusion, bf16[2,32,2,14,128,1]{4,1,3,2,0,5:T(8,128)(2,1)S(1)} %convert_bitcast_fusion), kind=kOutput, calls=%fused_computation.15 | convolution fusion | flops 469762048 | bytes 24576000 | tf_op jit(solution)/shard_map/cfaku,cfbsu->cfabsk/dot_general | solution.py:32
  210.8 8.2 %fusion.30 = f32[2,32,2,2,14,128]{5,4,2,3,1,0:T(8,128)S(1)} fusion(bf16[2,32,2,512,128]{4,3,2,1,0:T(8,128)(2,1)} %multiply_convert_fusion, bf16[2,32,1,14,512]{4,3,1,0,2:T(8,128)(2,1)S(1)} %fusion.39, bf16[2,32,1,14,512]{4,3,1,0,2:T(8,128)(2,1)S(1)} %fusion.38), kind=kOutput, calls=%fused_computation.36 | convolution fusion | flops 470679552 | bytes 20447232 | tf_op jit(solution)/shard_map/cfaku,cfbsk->cfabsu/dot_general | solution.py:24
  220.4 36.5 %all-gather.7.cloned.1.call-done = f32[4,32,2,14,128]{4,3,1,0,2:T(8,128)} async-done(((f32[2,32,2,14,128]{4,3,1,0,2:T(8,128)}), f32[4,32,2,14,128]{4,3,1,0,2:T(8,128)}) %all-gather.7.cloned.1.call-update) | async-done | bytes 1835024 | tf_op jit(solution)/shard_map/all_gather | solution.py:70
  257.0 2.9 reduce_sum.71
  266.1 7.0 %copy.157 = bf16[2,256,2,14,32]{4,2,3,0,1:T(2,128)(2,1)} copy(bf16[2,256,2,14,32]{1,0,4,3,2:T(2,128)(2,1)S(1)} %reshape.282) | data formatting | bytes 1835008 | tf_op jit(solution)/shard_map/reshape | solution.py:93
  273.2 5.1 %reshape.294 = bf16[2,2,114688]{2,1,0:T(2,128)(2,1)S(1)} reshape(bf16[256,2,14,2,32]{4,3,2,1,0:T(2,128)(2,1)} %bitcast.161) | data formatting | bytes 1835008
  278.2 4.5 %all_to_all.23 = bf16[2,2,114688]{2,1,0:T(2,128)(2,1)S(1)} all-to-all(bf16[2,2,114688]{2,1,0:T(2,128)(2,1)S(1)} %reshape.294), channel_id=1, replica_groups=mesh['cell'=2,'panel'=2,'sc'=32] {'cell'}, dimensions={0} | all-to-all | bytes 1835008 | tf_op jit(solution)/shard_map/all_to_all | solution.py:95
  282.7 3.0 reshape.295
  285.7 6.3 %bitcast_bitcast_fusion = bf16[256,2,14,2,32]{4,3,2,1,0:T(2,128)(2,1)} fusion(bf16[256,2,14,2,32]{4,3,2,1,0:T(2,128)(2,1)} %reshape.295), kind=kLoop, calls=%fused_computation.95 | loop fusion | bytes 1835008
  292.0 5.0 %reshape.296 = bf16[32,2,7168]{2,1,0:T(2,128)(2,1)S(1)} reshape(bf16[256,2,14,2,32]{4,3,2,1,0:T(2,128)(2,1)} %bitcast_bitcast_fusion) | data formatting | bytes 1835008
  297.0 27.4 %all_to_all.24 = bf16[32,2,7168]{2,1,0:T(2,128)(2,1)S(1)} all-to-all(bf16[32,2,7168]{2,1,0:T(2,128)(2,1)S(1)} %reshape.296), channel_id=1, replica_groups=mesh['cell'=2,'panel'=2,'sc'=32] {'sc'}, dimensions={0} | all-to-all | bytes 1835008 | tf_op jit(solution)/shard_map/all_to_all | solution.py:94
  324.4 3.2 reshape.297
  327.7 2.9 copy.227
  330.6 2.8 copy.180
  333.4 6.5 %reshape.293 = bf16[2,8,2,14,1024]{4,2,3,1,0:T(2,128)(2,1)} reshape(bf16[2,8,2,14,32,32]{5,4,2,3,1,0:T(8,128)(2,1)} %copy.180) | data formatting | bytes 1835008 | tf_op jit(solution)/shard_map/all_to_all | solution.py:94
  (48 shorter events, 31.0 us)
Async XLA Ops:
  6.5 57.8 %copy-start = (bf16[2,32,2,14,512]{4,2,3,1,0:T(2,128)(2,1)S(1)}, bf16[2,32,2,14,512]{4,2,3,1,0:T(2,128)(2,1)}, u32[]{:S(2)}) copy-start(bf16[2,32,2,14,512]{4,2,3,1,0:T(2,128)(2,1)} %param.6) | copy-start | bytes 5505028
  6.5 113.2 %all-reduce.2.cloned.1.call-start = ((), (), s32[]{:S(2)}) async-start(), calls=%async_computation.2 | async-start | bytes 1835008 | tf_op jit(solution)/shard_map/psum | solution.py:62
  8.7 16.5 %collective-permute-start = (bf16[2,1,2,512,128]{4,3,2,1,0:T(8,128)(2,1)}, bf16[2,1,2,512,128]{4,3,2,1,0:T(8,128)(2,1)S(1)}, u32[]{:S(2)}, u32[]{:S(2)}) collective-permute-start(bf16[2,1,2,512,128]{4,3,2,1,0:T(8,128)(2,1)} %get-tuple-element.7), channel_id=1, source_target_pairs={{0,1},{1,2},{2,3},{3,4},{4,5},{5,6},{6,7},{7,8},{8,9},{9,10},{10,1... | collective-permute-start | bytes 1572872 | tf_op jit(solution)/shard_map/ppermute | solution.py:15
  13.8 24.6 %collective-permute-start.1 = (bf16[2,1,2,512,128]{4,3,2,1,0:T(8,128)(2,1)S(1)}, bf16[2,1,2,512,128]{4,3,2,1,0:T(8,128)(2,1)S(1)}, u32[]{:S(2)}, u32[]{:S(2)}) collective-permute-start(bf16[2,1,2,512,128]{4,3,2,1,0:T(8,128)(2,1)S(1)} %get-tuple-element.8), channel_id=1, source_target_pairs={{1,0},{2,1},{3,2},{4,3},{5,4},{6,5},{7,6},{8,7},{9,8},{10,9},{11,1... | collective-permute-start | bytes 1572872 | tf_op jit(solution)/shard_map/ppermute | solution.py:18
  73.7 113.6 %all-gather.5.cloned.1.call-start = ((), (), s32[]{:S(2)}) async-start(), calls=%async_computation.3 | async-start | bytes 3145728 | tf_op jit(solution)/shard_map/all_gather | solution.py:70
  149.3 39.8 %copy-start.2 = (f32[2,32,2,14,128]{4,1,3,2,0:T(8,128)S(1)}, f32[2,32,2,14,128]{4,1,3,2,0:T(8,128)}, u32[]{:S(2)}) copy-start(f32[2,32,2,14,128]{4,1,3,2,0:T(8,128)} %all-reduce.2.cloned.1.call-done) | copy-start | bytes 2752516
  149.3 39.8 %copy-start.4 = (f32[2]{0:T(128)S(1)}, f32[2]{0:T(128)}, u32[]{:S(2)}) copy-start(f32[2]{0:T(128)} %param.7) | copy-start | bytes 28
  150.5 106.5 %all-gather.7.cloned.1.call-start = ((), (), s32[]{:S(2)}) async-start(), calls=%async_computation.4 | async-start | bytes 3145728 | tf_op jit(solution)/shard_map/all_gather | solution.py:70
  219.0 1.2 copy-start.3
  330.6 9.3 %copy-start.1 = (bf16[2,32,2,14,512]{4,2,3,1,0:T(2,128)(2,1)S(1)}, bf16[2,32,2,14,512]{4,2,3,1,0:T(2,128)(2,1)}, u32[]{:S(2)}) copy-start(bf16[2,32,2,14,512]{4,2,3,1,0:T(2,128)(2,1)} %param.6) | copy-start | bytes 5505028
Sparse Core Ops, SparseCore 0:
  73.8 45.8 all-reduce.1
  150.6 36.5 all-gather.4
  220.4 36.5 all-gather.6
